TPU v7x, 32 devices: a whole 2x2x4 slice. The times are simulated.
32 devices in a mesh: own: 8 (over z, y), rep: 4 (over x, core).
Axes of the slice: x: 2, y: 2, z: 4, core: 2. Of those that a mesh axis runs over, the one named last changes fastest.
Arguments:
- hidden: bfloat16 [1024, 1024], P('own', 'rep'), may hold values from -140 to 140
- weight: bfloat16 [8, 2048, 1024], P('own', None, 'rep'), may hold values from -0.1875 to 0.1875
- bucket_map: int32 [8], replicated, may hold values from 0 to 7, each once
- active: int32 [1024, 2], P('own'), may hold values from 0 to 7, all different within a row; in each aligned block of 128 rows (0 to 127, 128 to 255, ...) at most 64 rows name the same one
- label_pick: int32 [1024], P('own'), may hold values from 0 to 4095
Outputs:
- sample_loss: float32 [1024], P('own')
- grad_hidden: float32 [1024, 1024], P('own', 'rep')
- grad_weight: bfloat16 [8, 2048, 1024], P('own', None, 'rep')
Inputs may be any that keep to these rules, and one draw needn't show every extreme that they name: `bucket_map`: each weight slot is named once. `active`: A sample's 2 bucket ids differ. Among the 128 samples of one index of own, no bucket is named by more than 64 samples, a bound that some block reaches.
All inputs are finite; a program needn't handle non-finite values.
Results may differ from a plain program's by a relative error of at most 0.0032.
Values may be sent and summed in bfloat16 or wider, within the bound.
A program may use at most 64 MiB of HBM per device.

v0:
```python
import jax
import jax.numpy as jnp
from jax import lax
from jax.sharding import PartitionSpec as P


def body(hidden, weight, bucket_map, active, label_pick):
    samp_count = hidden.shape[0]
    bucket_dev, label_count, feature_part = weight.shape
    picks = active.shape[1]
    bucket_total = bucket_map.shape[0]
    owner_count = lax.axis_size("own")
    slot_depth = max(2, 2 * samp_count * picks // bucket_total)
    pair_count = samp_count * picks
    slots_total = bucket_total * slot_depth
    row_count = owner_count * slot_depth
    pair_bucket = active.reshape(pair_count)
    bucket_iota = lax.broadcasted_iota(jnp.int32, (pair_count, bucket_total), 1)
    slot_index = jnp.sum(
        jnp.where(pair_bucket[:, None] == bucket_iota, bucket_map[None, :], 0), axis=1
    )
    slot_hits = (slot_index[:, None] == bucket_iota).astype(jnp.int32)
    earlier = jnp.cumsum(slot_hits, axis=0) - slot_hits
    rank_within = jnp.sum(earlier * slot_hits, axis=1)
    position = slot_index * slot_depth + rank_within
    pair_index = jnp.arange(pair_count, dtype=jnp.int32)
    pick_value = jnp.repeat(label_pick, picks)
    target_pair = jnp.where(
        pick_value // label_count == pair_index % picks, pick_value % label_count, -1
    )
    width_sent = hidden.shape[1]
    pair_rows = jnp.repeat(hidden, picks, axis=0)
    send_rows = jnp.zeros((slots_total, width_sent), jnp.bfloat16).at[position].set(pair_rows)
    send_target = jnp.full((slots_total,), -1, jnp.int32).at[position].set(target_pair)
    got_rows, got_target = (
        lax.all_to_all(
            send_rows.reshape(owner_count, bucket_dev * slot_depth, width_sent),
            "own",
            split_axis=0,
            concat_axis=0,
            tiled=True,
        ),
        lax.all_to_all(
            send_target.reshape(owner_count, bucket_dev * slot_depth),
            "own",
            split_axis=0,
            concat_axis=0,
            tiled=True,
        ),
    )
    received = got_rows.reshape(owner_count, bucket_dev, slot_depth, width_sent).transpose(
        1, 0, 2, 3
    )
    received = received.reshape(bucket_dev, row_count, width_sent)
    target_col = (
        got_target.reshape(owner_count, bucket_dev, slot_depth)
        .transpose(1, 0, 2)
        .reshape(bucket_dev, row_count)
    )
    partial_value = jnp.einsum("brd,bcd->brc", received, weight, preferred_element_type=jnp.float32)
    logits = lax.psum(partial_value, "rep")
    columns = lax.broadcasted_iota(jnp.int32, (1, 1, label_count), 2)
    row_max = jnp.max(logits, axis=2)
    row_sum = jnp.sum(jnp.exp(logits - row_max[..., None]), axis=2)
    row_target = jnp.sum(jnp.where(columns == target_col[..., None], logits, 0.0), axis=2)

    def to_sources(values):
        return (
            values.reshape(bucket_dev, owner_count, slot_depth)
            .transpose(1, 0, 2)
            .reshape(owner_count, bucket_dev * slot_depth)
        )

    back_max, back_sum, back_target = (
        lax.all_to_all(to_sources(row_max), "own", split_axis=0, concat_axis=0, tiled=True),
        lax.all_to_all(to_sources(row_sum), "own", split_axis=0, concat_axis=0, tiled=True),
        lax.all_to_all(to_sources(row_target), "own", split_axis=0, concat_axis=0, tiled=True),
    )
    pair_max = back_max.reshape(slots_total)[position].reshape(samp_count, picks)
    pair_sum = back_sum.reshape(slots_total)[position].reshape(samp_count, picks)
    pair_target = back_target.reshape(slots_total)[position].reshape(samp_count, picks)
    peak_max = jnp.max(pair_max, axis=1)
    norm_sum = jnp.sum(pair_sum * jnp.exp(pair_max - peak_max[:, None]), axis=1)
    log_norm = peak_max + jnp.log(norm_sum)
    sample_loss = log_norm - jnp.sum(pair_target, axis=1)
    send_norm = jnp.zeros((slots_total,), jnp.float32).at[position].set(jnp.repeat(log_norm, picks))
    got_norm = lax.all_to_all(
        send_norm.reshape(owner_count, bucket_dev * slot_depth),
        "own",
        split_axis=0,
        concat_axis=0,
        tiled=True,
    )
    row_norm = (
        got_norm.reshape(owner_count, bucket_dev, slot_depth)
        .transpose(1, 0, 2)
        .reshape(bucket_dev, row_count)
    )
    onehot = (columns == target_col[..., None]).astype(jnp.float32)
    grad_logits = (jnp.exp(logits - row_norm[..., None]) - onehot).astype(jnp.bfloat16)
    grad_weight = jnp.einsum(
        "brc,brd->bcd", grad_logits, received, preferred_element_type=jnp.float32
    ).astype(jnp.bfloat16)
    row_grads = jnp.einsum("brc,bcd->brd", grad_logits, weight, preferred_element_type=jnp.float32)
    send_grads = row_grads.reshape(bucket_dev, owner_count, slot_depth, feature_part).transpose(
        1, 0, 2, 3
    )
    send_grads = send_grads.reshape(owner_count, bucket_dev * slot_depth, feature_part)
    got_grads = lax.all_to_all(send_grads, "own", split_axis=0, concat_axis=0, tiled=True)
    pair_grads = got_grads.reshape(slots_total, feature_part)[position].reshape(
        samp_count, picks, feature_part
    )
    grad_hidden = jnp.sum(pair_grads, axis=1)
    return (sample_loss, grad_hidden, grad_weight)


def solution(mesh):
    in_specs = (P("own", "rep"), P("own", None, "rep"), P(), P("own", None), P("own"))
    out_specs = (P("own"), P("own", "rep"), P("own", None, "rep"))
    return jax.shard_map(body, mesh=mesh, in_specs=in_specs, out_specs=out_specs, check_vma=False)
```

profile of v0, /device:TPU:0, one launch (start us, length us, event | category | flops | bytes accessed | tf_op | source)
XLA Modules:
  0.0 201.0 jit_solution(17374603025491268575)
XLA Ops:
  7.2 0.9 copy.8
  8.1 0.1 eq.66
  8.2 0.7 select_reduce_fusion.1
  9.0 0.6 reduce-window.6
  9.6 0.2 slice_reduce_fusion
  9.9 0.9 broadcast_in_dim.50
  10.9 1.5 scatter_custom_fusion
  12.5 16.0 %all_to_all.55 = bf16[8,64,256]{2,1,0:T(8,128)(2,1)S(1)} all-to-all(bf16[8,64,256]{2,1,0:T(8,128)(2,1)S(1)} %bitcast.33), channel_id=1, replica_groups=mesh['own'=8,'rep'=4] {'own'}, dimensions={0} | all-to-all | bytes 524288 | tf_op jit(solution)/shard_map/all_to_all | solution.py:36
  28.5 2.7 %convolution_bitcast_fusion = f32[1,512,2048]{2,1,0:T(8,128)} fusion(bf16[512,256]{1,0:T(8,128)(2,1)S(1)} %bitcast.34, bf16[1,2048,256]{2,1,0:T(8,128)(2,1)S(1)} %copy-done), kind=kOutput, calls=%fused_computation.11 | convolution fusion | flops 536870912 | bytes 5505024 | tf_op jit(solution)/shard_map/brd,bcd->brc/dot_general | solution.py:60
  31.3 0.1 reshape.229
  31.5 1.4 scatter_custom_fusion.1
  32.9 9.8 %all_to_all.56 = s32[8,1,64]{2,1,0:T(1,128)S(1)} all-to-all(s32[8,1,64]{2,1,0:T(1,128)S(1)} %all_to_all.41), channel_id=1, replica_groups=mesh['own'=8,'rep'=4] {'own'}, dimensions={0} | all-to-all | bytes 4096 | tf_op jit(solution)/shard_map/all_to_all | solution.py:43
  42.8 0.5 broadcast.131
  43.3 0.7 reduce.22
  44.0 71.8 %all-reduce.2.cloned.1.call-done = f32[1,512,2048]{2,1,0:T(8,128)} async-done(((f32[1,512,2048]{2,1,0:T(8,128)}), f32[1,512,2048]{2,1,0:T(8,128)}) %all-reduce.2.cloned.1.call-update) | async-done | bytes 4194320 | tf_op jit(solution)/shard_map/psum | solution.py:61
  115.8 2.5 %reduce_max.18 = f32[512]{0:T(512)S(1)} reduce(f32[1,512,2048]{2,1,0:T(8,128)} %all-reduce.2.cloned.1.call-done, f32[]{:T(128)} %constant.50.clone.1), dimensions={0,2}, to_apply=%region_6.7 | reduce | flops 1048064 | bytes 4196356 | tf_op jit(solution)/shard_map/reduce_max | solution.py:63
  118.3 3.6 %select_reduce_fusion = (f32[512]{0:T(512)S(1)}, f32[512]{0:T(512)S(1)}) fusion(f32[1,512,2048]{2,1,0:T(8,128)} %all-reduce.2.cloned.1.call-done, s32[512]{0:T(512)S(1)} %eq.76, f32[512]{0:T(512)S(1)} %reduce_max.18), kind=kLoop, calls=%fused_computation.8 | loop fusion | flops 5241856 | bytes 4202496 | tf_op jit(solution)/shard_map/reduce_sum | solution.py:65
  121.9 0.7 all_to_all.39
  122.6 5.5 %all-to-all-start.2 = ((f32[8,1,64]{2,1,0:T(1,128)}), f32[8,1,64]{2,1,0:T(1,128)S(1)}, u32[]{:S(2)}, u32[]{:S(2)}) async-start(f32[8,1,64]{2,1,0:T(1,128)} %all_to_all.39), calls=%async_computation.2 | async-start | bytes 8192 | tf_op jit(solution)/shard_map/all_to_all | solution.py:76
  128.1 0.7 all_to_all.37
  128.8 5.7 %all-to-all-done.2 = f32[8,1,64]{2,1,0:T(1,128)S(1)} async-done(((f32[8,1,64]{2,1,0:T(1,128)}), f32[8,1,64]{2,1,0:T(1,128)S(1)}, u32[]{:S(2)}, u32[]{:S(2)}) %all-to-all-start.2) | async-done | bytes 2080 | tf_op jit(solution)/shard_map/all_to_all | solution.py:76
  134.5 3.3 %all-to-all-start.1 = ((f32[8,1,64]{2,1,0:T(1,128)}), f32[8,1,64]{2,1,0:T(1,128)S(1)}, u32[]{:S(2)}, u32[]{:S(2)}) async-start(f32[8,1,64]{2,1,0:T(1,128)} %all_to_all.37), calls=%async_computation.1 | async-start | bytes 8192 | tf_op jit(solution)/shard_map/all_to_all | solution.py:75
  137.8 0.7 all_to_all.43
  138.5 5.7 %all-to-all-done.1 = f32[8,1,64]{2,1,0:T(1,128)S(1)} async-done(((f32[8,1,64]{2,1,0:T(1,128)}), f32[8,1,64]{2,1,0:T(1,128)S(1)}, u32[]{:S(2)}, u32[]{:S(2)}) %all-to-all-start.1) | async-done | bytes 2080 | tf_op jit(solution)/shard_map/all_to_all | solution.py:75
  144.2 3.3 %all-to-all-start.4 = ((f32[8,1,64]{2,1,0:T(1,128)}), f32[8,1,64]{2,1,0:T(1,128)S(1)}, u32[]{:S(2)}, u32[]{:S(2)}) async-start(f32[8,1,64]{2,1,0:T(1,128)} %all_to_all.43), calls=%async_computation.4 | async-start | bytes 8192 | tf_op jit(solution)/shard_map/all_to_all | solution.py:77
  147.5 0.5 broadcast.129
  148.0 0.7 reduce.21
  148.7 1.9 gather_fusion.1
  150.7 0.1 reshape.228
  150.8 0.7 reduce.20
  151.6 1.9 gather_fusion
  153.8 0.7 reduce.23
  154.5 1.9 gather_fusion.2
  156.6 0.2 multiply_reduce_fusion
  156.9 0.5 fusion.14
  157.5 0.1 reshape.288
  157.7 1.4 scatter_custom_fusion.2
  159.2 12.2 %all_to_all.57 = f32[8,1,64]{2,1,0:T(1,128)S(1)} all-to-all(f32[8,1,64]{2,1,0:T(1,128)S(1)} %all_to_all.45), channel_id=1, replica_groups=mesh['own'=8,'rep'=4] {'own'}, dimensions={0} | all-to-all | bytes 4096 | tf_op jit(solution)/shard_map/all_to_all | solution.py:87
  171.4 0.7 reduce.24
  172.1 3.3 %subtract_convert_fusion = bf16[1,512,2048]{2,1,0:T(8,128)(2,1)S(1)} fusion(f32[1,512,2048]{2,1,0:T(8,128)} %all-reduce.2.cloned.1.call-done, f32[512]{0:T(512)S(1)} %sub.48, s32[512]{0:T(512)S(1)} %eq.76), kind=kLoop, calls=%fused_computation.7 | loop fusion | flops 5242880 | bytes 6295552 | tf_op jit(solution)/shard_map/convert_element_type | solution.py:100
  175.4 1.3 copy-done.1
  176.8 1.5 fusion.2
  178.3 3.5 %all-to-all-start.6 = ((f32[8,64,256]{2,1,0:T(8,128)}), f32[8,64,256]{2,1,0:T(8,128)S(1)}, u32[]{:S(2)}, u32[]{:S(2)}) async-start(f32[8,64,256]{2,1,0:T(8,128)} %fusion.2), calls=%async_computation.6 | async-start | bytes 1048576 | tf_op jit(solution)/shard_map/all_to_all | solution.py:109
  181.8 3.3 %fusion = bf16[1,2048,256]{2,1,0:T(8,128)(2,1)} fusion(bf16[512,256]{1,0:T(8,128)(2,1)S(1)} %bitcast.35, bf16[1,512,2048]{2,1,0:T(8,128)(2,1)} %copy-done.1), kind=kOutput, calls=%fused_computation.13 | convolution fusion | flops 537395200 | bytes 3407872 | tf_op jit(solution)/shard_map/brc,brd->bcd/dot_general | solution.py:101
  185.1 6.9 %all-to-all-done.6 = f32[8,64,256]{2,1,0:T(8,128)S(1)} async-done(((f32[8,64,256]{2,1,0:T(8,128)}), f32[8,64,256]{2,1,0:T(8,128)S(1)}, u32[]{:S(2)}, u32[]{:S(2)}) %all-to-all-start.6) | async-done | bytes 524320 | tf_op jit(solution)/shard_map/all_to_all | solution.py:109
  192.0 1.0 gather_fusion.3
  193.0 0.1 reshape.234
  193.2 1.0 reduce_sum.69
  (30 shorter events, 1.5 us)
Async XLA Ops:
  7.2 21.3 %copy-start = (bf16[1,2048,256]{2,1,0:T(8,128)(2,1)S(1)}, bf16[1,2048,256]{2,1,0:T(8,128)(2,1)}, u32[]{:S(2)}) copy-start(bf16[1,2048,256]{2,1,0:T(8,128)(2,1)} %param.6) | copy-start | bytes 3145732
  7.2 108.6 %all-reduce.2.cloned.1.call-start = ((), (), s32[]{:S(2)}) async-start(), calls=%async_computation.7 | async-start | bytes 8388608 | tf_op jit(solution)/shard_map/psum | solution.py:61
  28.5 2.7 %copy-start.2 = (s32[128]{0:T(128)S(1)}, s32[128]{0:T(128)}, u32[]{:S(2)}) copy-start(s32[128]{0:T(128)} %param.9) | copy-start | bytes 1540
  122.6 11.9 %all-to-all-start.2 = ((f32[8,1,64]{2,1,0:T(1,128)}), f32[8,1,64]{2,1,0:T(1,128)S(1)}, u32[]{:S(2)}, u32[]{:S(2)}) async-start(f32[8,1,64]{2,1,0:T(1,128)} %all_to_all.39), calls=%async_computation.2 | async-start | bytes 8192 | tf_op jit(solution)/shard_map/all_to_all | solution.py:76
  134.5 9.6 %all-to-all-start.1 = ((f32[8,1,64]{2,1,0:T(1,128)}), f32[8,1,64]{2,1,0:T(1,128)S(1)}, u32[]{:S(2)}, u32[]{:S(2)}) async-start(f32[8,1,64]{2,1,0:T(1,128)} %all_to_all.37), calls=%async_computation.1 | async-start | bytes 8192 | tf_op jit(solution)/shard_map/all_to_all | solution.py:75
  144.2 9.6 %all-to-all-start.4 = ((f32[8,1,64]{2,1,0:T(1,128)}), f32[8,1,64]{2,1,0:T(1,128)S(1)}, u32[]{:S(2)}, u32[]{:S(2)}) async-start(f32[8,1,64]{2,1,0:T(1,128)} %all_to_all.43), calls=%async_computation.4 | async-start | bytes 8192 | tf_op jit(solution)/shard_map/all_to_all | solution.py:77
  175.4 1.4 copy-start.1
  178.3 13.7 %all-to-all-start.6 = ((f32[8,64,256]{2,1,0:T(8,128)}), f32[8,64,256]{2,1,0:T(8,128)S(1)}, u32[]{:S(2)}, u32[]{:S(2)}) async-start(f32[8,64,256]{2,1,0:T(8,128)} %fusion.2), calls=%async_computation.6 | async-start | bytes 1048576 | tf_op jit(solution)/shard_map/all_to_all | solution.py:109
Sparse Core Ops, SparseCore 0:
  31.3 84.4 all-reduce.1
where the time goes:
time: 202 us; the launch traced here: 201 us
  waiting for transfers between devices  90.1 us (45%)
  blocking collectives  38 us (19%)
  local copies, waits for them, and re-layouts  19.3 us (10%)
  other arithmetic  16.1 us (8%)
  starting transfers between devices  15.7 us (8%)
  between operations  14.3 us (7%)
  matrix products  7.55 us (4%)
    psum x1, waiting for transfers between devices, body(): logits = lax.psum(partial_value, 'rep')  71.8 us
    all_to_all x1, blocking collectives, body(): lax.all_to_all(send_rows.reshape(owner_count, bucket_dev * slot_depth, wi...  16 us
    all_to_all x1, blocking collectives, body(): lax.all_to_all(send_norm.reshape(owner_count, bucket_dev * slot_depth), '...  12.2 us
    all_to_all x1, blocking collectives, body(): lax.all_to_all(send_target.reshape(owner_count, bucket_dev * slot_depth),...  9.84 us
    all_to_all x1, waiting for transfers between devices, body(): lax.all_to_all(send_grads, 'own', split_axis=0, concat_axis=0, tiled=True)  6.92 us
    all_to_all x1, waiting for transfers between devices, body(): lax.all_to_all(to_sources(row_sum), 'own', split_axis=0, concat_axis=0, t...  5.72 us
    all_to_all x1, waiting for transfers between devices, body(): lax.all_to_all(to_sources(row_max), 'own', split_axis=0, concat_axis=0, t...  5.65 us
    all_to_all x1, starting transfers between devices, body(): lax.all_to_all(to_sources(row_sum), 'own', split_axis=0, concat_axis=0, t...  5.52 us
  transfers between devices with their start and end apart: 5, of which 4 were waited for; matrix products, arithmetic and copies ran while one was open for 6% of the time, Pallas kernels for 0%

commit v1 on v0

--- a/solution.py
+++ b/solution.py
@@ -1,7 +1,323 @@
+import functools
 import jax
 import jax.numpy as jnp
 from jax import lax
+from jax.experimental import pallas as pl
+from jax.experimental.pallas import tpu as pltpu
 from jax.sharding import PartitionSpec as P
+
+MESH = pl.DeviceIdType.MESH
+F32 = jnp.float32
+BF16 = jnp.bfloat16
+NT = (((1,), (1,)), ((), ()))
+TN = (((0,), (0,)), ((), ()))
+
+
+def ranks(slot0, slot1, buckets, upper):
+    sources, samples = slot0.shape
+    bucket = lax.broadcasted_iota(jnp.int32, (buckets, samples), 0)
+    hits = [
+        jnp.where((slot0[s : s + 1] == bucket) | (slot1[s : s + 1] == bucket), 1.0, 0.0)
+        for s in range(sources)
+    ]
+    hits = jnp.concatenate(hits, axis=0) if sources > 1 else hits[0]
+    earlier = jnp.dot(hits.astype(BF16), upper, preferred_element_type=F32)
+    return jnp.where(hits > 0.5, earlier, -1.0).astype(jnp.int32)
+
+
+def lane_pick(values, index):
+    return jnp.take_along_axis(values, index, axis=1)
+
+
+def kernel(
+    n, depth, picks_labels, bmap, meta, hidden, weight,
+    loss_ref, gh_ref, gw_ref,
+    metas, wfull, sendbuf, rows, rinfo, lt, stats, statrep, comb, statown, norms, tsums,
+    g_all, gh_acc, ghsend, ghrecv,
+    s_meta, r_meta, s_w, r_w, s_row, r_row, s_fx, r_fx, s_fc, r_fc, s_fr, r_fr,
+    s_sr, r_sr, s_so, r_so, s_gx, r_gx, s_gc, r_gc, s_gr, r_gr, s_gh, r_gh,
+):
+    o = lax.axis_index("own")
+    r = lax.axis_index("rep")
+    p1 = r + 1 - 2 * lax.rem(r, 2)
+    p2 = lax.rem(r + 2, 4)
+    p3 = lax.rem(p1 + 2, 4)
+    labels, part = weight.shape
+    samples = hidden.shape[0]
+    cols = labels // 4
+    row_count = n * depth
+    pending = []
+
+    def send(src, dst, ssem, rsem, own, rep):
+        copy = pltpu.make_async_remote_copy(
+            src_ref=src, dst_ref=dst, send_sem=ssem, recv_sem=rsem,
+            device_id={"own": own, "rep": rep}, device_id_type=MESH,
+        )
+        copy.start()
+        pending.append(copy)
+        return copy
+
+    def at_rows(s):
+        return pl.ds(pl.multiple_of(s * depth, depth), depth)
+
+    def at_part(q):
+        return pl.ds(pl.multiple_of(q * part, part), part)
+
+    def at_cols(q, c=0, size=None):
+        size = cols if size is None else size
+        return pl.ds(pl.multiple_of(q * cols + c * size, size), size)
+
+    barrier = pltpu.get_barrier_semaphore()
+    for k in range(1, n):
+        pl.semaphore_signal(barrier, inc=1, device_id={"own": lax.rem(o + k, n), "rep": r}, device_id_type=MESH)
+    for q in (p1, p2, p3):
+        pl.semaphore_signal(barrier, inc=1, device_id={"own": o, "rep": q}, device_id_type=MESH)
+    pl.semaphore_wait(barrier, n - 1 + 3)
+
+    w_copies = [
+        send(weight.at[at_cols(q)], wfull.at[:, at_part(r)], s_w.at[i], r_w.at[i], o, q)
+        for i, q in ((1, p2), (2, p3), (0, p1))
+    ]
+    meta_copies = [
+        send(meta, metas.at[o], s_meta.at[k - 1], r_meta.at[k - 1], lax.rem(o + k, n), r)
+        for k in range(1, n)
+    ]
+
+    below = lax.broadcasted_iota(jnp.int32, (samples, samples), 0)
+    right = lax.broadcasted_iota(jnp.int32, (samples, samples), 1)
+    upper = jnp.where(below < right, 1.0, 0.0).astype(BF16)
+
+    def slots(ids):
+        out = jnp.zeros_like(ids)
+        for b in range(n):
+            out = jnp.where(ids == b, bmap[b], out)
+        return out
+
+    mine = meta[...]
+    own_rank = ranks(slots(mine[0:1]), slots(mine[1:2]), n, upper)
+    place = lax.broadcasted_iota(jnp.int32, (depth, samples), 0)
+    pack = jnp.concatenate(
+        [jnp.where(own_rank[b : b + 1] == place, 1.0, 0.0).astype(BF16) for b in range(n)], axis=0
+    )
+    packed = jnp.dot(pack, hidden[...], preferred_element_type=F32).astype(BF16)
+    for b in range(n):
+        sendbuf[b] = packed[b * depth : (b + 1) * depth]
+    row_copies = [
+        send(sendbuf.at[lax.rem(o + k, n)], rows.at[at_rows(o), at_part(r)], s_row.at[k - 1], r_row.at[k - 1], lax.rem(o + k, n), r)
+        for k in range(1, n)
+    ]
+    rows[at_rows(o), at_part(r)] = sendbuf[o]
+    wfull[:, at_part(r)] = weight[at_cols(r), :]
+    metas[o] = mine
+
+    fx, fc, fr = [], [], []
+    for k in range(n):
+        s = lax.rem(o - k + n, n)
+        if k > 0:
+            row_copies[k - 1].wait_recv()
+        block = rows.at[at_rows(s), at_part(r)]
+        fx.append(send(block, block, s_fx.at[k], r_fx.at[k], o, p2))
+        fc.append(send(block, block, s_fc.at[k], r_fc.at[k], o, p1))
+
+    for c in meta_copies:
+        c.wait_recv()
+    slot0 = slots(metas[:, 0, :])
+    slot1 = slots(metas[:, 1, :])
+    pick = metas[:, 2, :]
+    rank_all = ranks(slot0, slot1, n, upper)
+    wanted = jnp.where(pick < labels, slot0, slot1)
+    code = jnp.where(wanted == o, jnp.where(pick < labels, pick, pick - labels) + 1, 0)
+    code_hi = (code // 64).astype(F32)
+    code_lo = (code - (code // 64) * 64).astype(F32)
+    lane = lax.broadcasted_iota(jnp.int32, (1, samples), 1)
+    sub = lax.broadcasted_iota(jnp.int32, (8, samples), 0)
+    bucket_sub = lax.broadcasted_iota(jnp.int32, (n, samples), 0)
+    infos = []
+    place2 = lax.broadcasted_iota(jnp.int32, (2 * depth, samples), 0)
+    for sp in range(n // 2):
+        info = jnp.zeros((8, 2 * depth), F32)
+        for h in range(2):
+            s = 2 * sp + h
+            rank_me = jnp.max(
+                jnp.where(bucket_sub == o, rank_all[s * n : (s + 1) * n], -1), axis=0, keepdims=True
+            )
+            member = jnp.where(
+                (rank_me >= 0) & (rank_me + h * depth == place2), 1.0, 0.0
+            ).astype(BF16)
+            facts = jnp.where(
+                sub == 0, lane.astype(F32),
+                jnp.where(sub == 1, code_hi[s : s + 1], jnp.where(sub == 2, code_lo[s : s + 1], jnp.where(sub == 3, 1.0, 0.0))),
+            ).astype(BF16)
+            info = info + lax.dot_general(facts, member, NT, preferred_element_type=F32)
+        infos.append(info)
+    row_index = [x[0:1].astype(jnp.int32) for x in infos]
+    row_valid = jnp.concatenate([x[3:4] for x in infos], axis=1) > 0.5
+    row_target = jnp.concatenate([(x[1:2] * 64.0 + x[2:3]) for x in infos], axis=1).astype(jnp.int32) - 1
+
+    for k in range(n):
+        fx[k].wait_recv()
+        s = lax.rem(o - k + n, n)
+        block = rows.at[at_rows(s), at_part(p2)]
+        fr.append(send(block, block, s_fr.at[k], r_fr.at[k], o, p1))
+    for k in range(n):
+        fc[k].wait_recv()
+    for c in w_copies:
+        c.wait_recv()
+    for k in range(n):
+        fr[k].wait_recv()
+
+    logits = lax.dot_general(wfull[...], rows[...], NT, preferred_element_type=F32)
+    top = jnp.max(logits, axis=0, keepdims=True)
+    label_id = lax.broadcasted_iota(jnp.int32, (cols, row_count), 0) + r * cols
+    hot = label_id == row_target
+    target_sum = jnp.sum(jnp.where(hot, logits, 0.0), axis=0, keepdims=True)
+    raised = jnp.exp(logits - top)
+    lt[...] = raised
+    lse = top + jnp.log(jnp.sum(raised, axis=0, keepdims=True))
+    for sp in range(n // 2):
+        stats[sp : sp + 1, :] = lse[:, sp * 128 : (sp + 1) * 128]
+        stats[n // 2 + sp : n // 2 + sp + 1, :] = target_sum[:, sp * 128 : (sp + 1) * 128]
+    sr = [
+        send(stats, statrep.at[r], s_sr.at[i], r_sr.at[i], o, q)
+        for i, q in ((1, p2), (2, p3), (0, p1))
+    ]
+    statrep[r] = stats[...]
+    for c in sr:
+        c.wait_recv()
+    parts = [statrep[q] for q in range(4)]
+    high = jnp.maximum(jnp.maximum(parts[0], parts[1]), jnp.maximum(parts[2], parts[3]))
+    total = high + jnp.log(sum(jnp.exp(x - high) for x in parts))
+    is_lse = lax.broadcasted_iota(jnp.int32, (n, samples), 0) < n // 2
+    comb[...] = jnp.where(is_lse, total, sum(parts))
+    so = [
+        send(comb, statown.at[o], s_so.at[k - 1], r_so.at[k - 1], lax.rem(o + k, n), r)
+        for k in range(1, n)
+    ]
+    statown[o] = comb[...]
+    for c in so:
+        c.wait_recv()
+    norm_rows = []
+    for sp in range(n // 2):
+        held = statown[:, sp, :]
+        pair = []
+        for h in range(2):
+            s = 2 * sp + h
+            rank = rank_all[s * n : (s + 1) * n]
+            index = jnp.where(rank >= 0, rank + h * depth, 0)
+            value = jnp.where(rank >= 0, lane_pick(held, index), -3.0e38)
+            most = jnp.max(value, axis=0, keepdims=True)
+            norm = most + jnp.log(jnp.sum(jnp.exp(value - most), axis=0, keepdims=True))
+            norms[s : s + 1, :] = norm
+            pair.append(
+                lane_pick(jnp.broadcast_to(norm, (8, samples)), jnp.broadcast_to(row_index[sp], (8, samples)))[0:1]
+            )
+        norm_rows.append(jnp.where(lane < depth, pair[0], pair[1]))
+    row_norm = jnp.concatenate(norm_rows, axis=1)
+    scale = jnp.where(row_valid, jnp.exp(top - row_norm), 0.0)
+
+    chunk = cols // 4
+    gx, gc, gr = [], [], []
+    for c in range(4):
+        ids = lax.broadcasted_iota(jnp.int32, (chunk, row_count), 0) + (r * cols + c * chunk)
+        grad = lt[c * chunk : (c + 1) * chunk, :] * scale - jnp.where(ids == row_target, 1.0, 0.0)
+        g_all[at_cols(r, c, chunk), :] = grad.astype(BF16)
+        block = g_all.at[at_cols(r, c, chunk)]
+        gx.append(send(block, block, s_gx.at[c], r_gx.at[c], o, p2))
+        gc.append(send(block, block, s_gc.at[c], r_gc.at[c], o, p1))
+
+    for sp in range(n // 2):
+        held = statown[:, n // 2 + sp, :]
+        for h in range(2):
+            s = 2 * sp + h
+            rank = rank_all[s * n : (s + 1) * n]
+            index = jnp.where(rank >= 0, rank + h * depth, 0)
+            value = jnp.where(rank >= 0, lane_pick(held, index), 0.0)
+            tsums[s : s + 1, :] = jnp.sum(value, axis=0, keepdims=True)
+    loss_ref[...] = norms[pl.ds(o, 1), :] - tsums[pl.ds(o, 1), :]
+
+    def row_term(q):
+        return lax.dot_general(g_all[at_cols(q), :], weight[at_cols(q), :], TN, preferred_element_type=F32)
+
+    def weight_term(q):
+        gw_ref[at_cols(q), :] = jnp.dot(
+            g_all[at_cols(q), :], rows[:, at_part(r)], preferred_element_type=F32
+        ).astype(BF16)
+
+    gh_acc[...] = row_term(r)
+    weight_term(r)
+    for c in range(4):
+        gx[c].wait_recv()
+        block = g_all.at[at_cols(p2, c, chunk)]
+        gr.append(send(block, block, s_gr.at[c], r_gr.at[c], o, p1))
+    for c in range(4):
+        gc[c].wait_recv()
+    gh_acc[...] += row_term(p1)
+    gh_acc[...] += row_term(p2)
+    for c in range(4):
+        gr[c].wait_recv()
+    ghsend[...] = (gh_acc[...] + row_term(p3)).astype(BF16)
+    back = [
+        send(ghsend.at[at_rows(lax.rem(o + k, n))], ghrecv.at[at_rows(o)], s_gh.at[k - 1], r_gh.at[k - 1], lax.rem(o + k, n), r)
+        for k in range(1, n)
+    ]
+    ghrecv[at_rows(o), :] = ghsend[at_rows(o), :]
+    weight_term(p1)
+    weight_term(p2)
+    weight_term(p3)
+    for c in back:
+        c.wait_recv()
+    gh_ref[...] = lax.dot_general(pack, ghrecv[...], TN, preferred_element_type=F32)
+    for c in pending:
+        c.wait_send()
+
+
+def fused(hidden, weight, bucket_map, active, label_pick):
+    samples, part = hidden.shape
+    labels = weight.shape[1]
+    n = bucket_map.shape[0]
+    depth = 2 * samples * active.shape[1] // n
+    cols = labels // 4
+    row_count = n * depth
+    meta = jnp.concatenate(
+        [active.T, label_pick[None], jnp.zeros((5, samples), jnp.int32)], axis=0
+    )
+    vmem = pl.BlockSpec(memory_space=pltpu.VMEM)
+    dma = pltpu.SemaphoreType.DMA
+    sems = []
+    for count in (n - 1, 3, n - 1, n, n, n, 3, n - 1, 4, 4, 4, n - 1):
+        sems += [dma((count,)), dma((count,))]
+    loss, grad_hidden, grad_weight = pl.pallas_call(
+        functools.partial(kernel, n, depth, labels),
+        out_shape=(
+            jax.ShapeDtypeStruct((1, samples), F32),
+            jax.ShapeDtypeStruct((samples, part), F32),
+            jax.ShapeDtypeStruct((labels, part), BF16),
+        ),
+        in_specs=[pl.BlockSpec(memory_space=pltpu.SMEM), vmem, vmem, vmem],
+        out_specs=(vmem, vmem, vmem),
+        scratch_shapes=[
+            pltpu.VMEM((n, 8, samples), jnp.int32),
+            pltpu.VMEM((cols, 4 * part), BF16),
+            pltpu.VMEM((n, depth, part), BF16),
+            pltpu.VMEM((row_count, 4 * part), BF16),
+            pltpu.VMEM((8, row_count), F32),
+            pltpu.VMEM((cols, row_count), F32),
+            pltpu.VMEM((n, samples), F32),
+            pltpu.VMEM((4, n, samples), F32),
+            pltpu.VMEM((n, samples), F32),
+            pltpu.VMEM((n, n, samples), F32),
+            pltpu.VMEM((n, samples), F32),
+            pltpu.VMEM((n, samples), F32),
+            pltpu.VMEM((labels, row_count), BF16),
+            pltpu.VMEM((row_count, part), F32),
+            pltpu.VMEM((row_count, part), BF16),
+            pltpu.VMEM((row_count, part), BF16),
+        ] + sems,
+        compiler_params=pltpu.CompilerParams(
+            collective_id=0, has_side_effects=True, vmem_limit_bytes=48 * 1024 * 1024
+        ),
+    )(bucket_map, meta, hidden, weight[0])
+    return loss[0], grad_hidden, grad_weight[None]
 
 
 def body(hidden, weight, bucket_map, active, label_pick):
@@ -114,7 +430,25 @@
     return (sample_loss, grad_hidden, grad_weight)
 
 
+def choose(hidden, weight, bucket_map, active, label_pick):
+    samples, picks = active.shape
+    buckets = bucket_map.shape[0]
+    depth = 2 * samples * picks // buckets
+    fits = (
+        weight.shape[0] == 1
+        and lax.axis_size("rep") == 4
+        and buckets == 8
+        and picks == 2
+        and samples == 128
+        and 2 * depth == samples
+        and weight.shape[1] % 512 == 0
+        and hidden.shape[1] % 128 == 0
+    )
+    run = fused if fits else body
+    return run(hidden, weight, bucket_map, active, label_pick)
+
+
 def solution(mesh):
     in_specs = (P("own", "rep"), P("own", None, "rep"), P(), P("own", None), P("own"))
     out_specs = (P("own"), P("own", "rep"), P("own", None, "rep"))
-    return jax.shard_map(body, mesh=mesh, in_specs=in_specs, out_specs=out_specs, check_vma=False)
+    return jax.shard_map(choose, mesh=mesh, in_specs=in_specs, out_specs=out_specs, check_vma=False)

time: 202 us -> 60.7 us (0.30)
  waiting for transfers between devices: 90.1 us -> 0 us
  Pallas kernels: 0 us -> 53.3 us
  blocking collectives: 38 us -> 0 us
  other arithmetic: 16.1 us -> 0.07 us
  starting transfers between devices: 15.7 us -> 0 us
  local copies, waits for them, and re-layouts: 19.3 us -> 5.46 us
  between operations: 14.3 us -> 0.67 us
  matrix products: 7.55 us -> 0 us
    psum x1 -> x0, waiting for transfers between devices: 71.8 us -> none  [body(): logits = lax.psum(partial_value, 'rep')]
    pallas_call x0 -> x1, Pallas kernels: none -> 53.3 us  [fused(): pl.pallas_call(functools.partial(kernel, n, depth, labels), out_shape=(ja...]
    all_to_all x3 -> x0, blocking collectives: 38 us -> none  [the longest x1 16 us: body(): lax.all_to_all(send_rows.reshape(owner_count, bucket_dev * slot_depth, wi...]
    all_to_all x4 -> x0, waiting for transfers between devices: 18.3 us -> none  [the longest x1 6.92 us: body(): lax.all_to_all(send_grads, 'own', split_axis=0, concat_axis=0, tiled=True)]
    all_to_all x4 -> x0, starting transfers between devices: 15.6 us -> none  [the longest x1 5.52 us: body(): lax.all_to_all(to_sources(row_sum), 'own', split_axis=0, concat_axis=0, t...]
    dot_general x3 -> x0, matrix products: 7.55 us -> none  [the longest x1 3.32 us: body(): jnp.einsum('brc,brd->bcd', grad_logits, received, preferred_element_type=...]
    gather x4 -> x0, local copies, waits for them, and re-layouts: 6.8 us -> none  [the longest x1 1.94 us: body(): back_sum.reshape(slots_total)[position].reshape(samp_count, picks)]
    reduce_sum x6 -> x0, other arithmetic: 5.72 us -> none  [the longest x1 3.64 us: body(): jnp.sum(jnp.where(columns == target_col[..., None], logits, 0.0), axis=2)]
  transfers between devices with their start and end apart: 5 -> 0, of which waited for: 4 -> 0; matrix products, arithmetic and copies ran while one was open for 6% -> 0% of each run, Pallas kernels for 0% -> 0%
where the time goes in v1:
time: 60.7 us; the launch traced here: 59.5 us
  Pallas kernels  53.3 us (88%)
  local copies, waits for them, and re-layouts  5.46 us (9%)
  between operations  0.67 us (1%)
    pallas_call x1, Pallas kernels, fused(): pl.pallas_call(functools.partial(kernel, n, depth, labels), out_shape=(ja...  53.3 us
    unnamed x13, local copies, waits for them, and re-layouts  5.38 us

profile of v1, /device:TPU:0, one launch (start us, length us, event | category | flops | bytes accessed | tf_op | source)
XLA Modules:
  0.0 59.5 jit_solution(3854276526553285452)
XLA Ops:
  0.6 0.0 copy-start.3
  0.7 0.0 copy-start.4
  0.7 0.1 pad.2.clone
  0.7 0.6 copy-done.3
  1.3 0.0 copy-done.4
  1.3 0.0 copy-start.2
  1.3 0.1 add_add_fusion.meta
  1.4 0.6 copy-done.2
  2.0 0.0 copy-start
  2.0 1.2 %copy-done = bf16[1,2048,256]{2,1,0:T(8,128)(2,1)S(1)} copy-done((bf16[1,2048,256]{2,1,0:T(8,128)(2,1)S(1)}, bf16[1,2048,256]{2,1,0:T(8,128)(2,1)}, u32[]{:S(2)}) %copy-start) | copy-done | bytes 1048600
  3.2 0.0 copy-start.1
  3.2 0.8 %copy-done.1 = bf16[128,256]{1,0:T(8,128)(2,1)S(1)} copy-done((bf16[128,256]{1,0:T(8,128)(2,1)S(1)}, bf16[128,256]{1,0:T(8,128)(2,1)}, u32[]{:S(2)}) %copy-start.1) | copy-done | bytes 65560
  4.0 53.3 %shard_map.76 = (f32[1,128]{1,0:T(1,128)S(1)}, f32[128,256]{1,0:T(8,128)S(1)}, bf16[2048,256]{1,0:T(8,128)(2,1)S(1)}) custom-call(s32[8]{0:T(128)S(1)} %copy-done.2, s32[8,128]{1,0:T(8,128)S(1)} %add_add_fusion.meta, bf16[128,256]{1,0:T(8,128)(2,1)S(1)} %copy-done.1, bf16[2048,256]{1,0:T(8,128)(2,1)S(1)} %bitcast.5), custom_call_target="tpu_custom_call" | custom-call | tf_op jit(solution)/shard_map/pallas_call | solution.py:289
  57.4 0.5 copy.11
  57.9 0.7 %copy.12 = f32[128,256]{1,0:T(8,128)} copy(f32[128,256]{1,0:T(8,128)S(1)} %get-tuple-element.13) | data formatting | bytes 262144
  58.6 1.0 %copy.13 = bf16[1,2048,256]{2,1,0:T(8,128)(2,1)} copy(bf16[1,2048,256]{2,1,0:T(8,128)(2,1)S(1)} %bitcast.6) | data formatting | bytes 2097152
  (1 shorter events, 0.0 us)
Async XLA Ops:
  0.6 0.7 %copy-start.3 = (s32[128,2]{0,1:T(2,128)S(1)}, s32[128,2]{0,1:T(2,128)}, u32[]{:S(2)}) copy-start(s32[128,2]{0,1:T(2,128)} %param.8) | copy-start | bytes 3076
  0.7 0.7 %copy-start.4 = (s32[128]{0:T(128)S(1)}, s32[128]{0:T(128)}, u32[]{:S(2)}) copy-start(s32[128]{0:T(128)} %param.9) | copy-start | bytes 1540
  1.3 0.7 %copy-start.2 = (s32[8]{0:T(128)S(1)}, s32[8]{0:T(128)}, u32[]{:S(2)}) copy-start(s32[8]{0:T(128)} %bmap.1) | copy-start | bytes 100
  2.0 1.2 %copy-start = (bf16[1,2048,256]{2,1,0:T(8,128)(2,1)S(1)}, bf16[1,2048,256]{2,1,0:T(8,128)(2,1)}, u32[]{:S(2)}) copy-start(bf16[1,2048,256]{2,1,0:T(8,128)(2,1)} %param.6) | copy-start | bytes 3145732
  3.2 0.8 %copy-start.1 = (bf16[128,256]{1,0:T(8,128)(2,1)S(1)}, bf16[128,256]{1,0:T(8,128)(2,1)}, u32[]{:S(2)}) copy-start(bf16[128,256]{1,0:T(8,128)(2,1)} %hidden.1) | copy-start | bytes 196612

commit v2 on v1

--- a/solution.py
+++ b/solution.py
@@ -30,23 +30,33 @@
 
 
 def kernel(
-    n, depth, picks_labels, bmap, meta, hidden, weight,
-    loss_ref, gh_ref, gw_ref,
-    metas, wfull, sendbuf, rows, rinfo, lt, stats, statrep, comb, statown, norms, tsums,
-    g_all, gh_acc, ghsend, ghrecv,
-    s_meta, r_meta, s_w, r_w, s_row, r_row, s_fx, r_fx, s_fc, r_fc, s_fr, r_fr,
+    n, depth, meta_hbm, hidden_hbm, weight_hbm,
+    loss_ref, gh_ref, gw_hbm,
+    meta, hidden, hidden_x, weight, metas, wfull, sendbuf, sendbuf_x, rows, stats, statrep, comb, statown,
+    norms, tsums, e_all, g_all, gh_acc, ghsend, ghrecv, gw_ref,
+    s_loc, s_hx, r_hx, s_meta, r_meta, s_w, r_w, s_row, r_row, s_rowx, r_rowx, s_fc, r_fc, s_fr, r_fr,
     s_sr, r_sr, s_so, r_so, s_gx, r_gx, s_gc, r_gc, s_gr, r_gr, s_gh, r_gh,
 ):
+    labels, part = weight_hbm.shape
+    samples = hidden_hbm.shape[0]
+    cols = labels // 4
     o = lax.axis_index("own")
     r = lax.axis_index("rep")
     p1 = r + 1 - 2 * lax.rem(r, 2)
     p2 = lax.rem(r + 2, 4)
     p3 = lax.rem(p1 + 2, 4)
-    labels, part = weight.shape
-    samples = hidden.shape[0]
-    cols = labels // 4
     row_count = n * depth
     pending = []
+    local = [
+        pltpu.make_async_copy(meta_hbm, meta, s_loc.at[0]),
+        pltpu.make_async_copy(hidden_hbm, hidden, s_loc.at[1]),
+        pltpu.make_async_copy(weight_hbm, weight, s_loc.at[2]),
+        pltpu.make_async_copy(
+            weight_hbm.at[pl.ds(pl.multiple_of(r * cols, cols), cols)],
+            wfull.at[:, pl.ds(pl.multiple_of(r * part, part), part)],
+            s_loc.at[3],
+        ),
+    ]
 
     def send(src, dst, ssem, rsem, own, rep):
         copy = pltpu.make_async_remote_copy(
@@ -72,26 +82,17 @@
         pl.semaphore_signal(barrier, inc=1, device_id={"own": lax.rem(o + k, n), "rep": r}, device_id_type=MESH)
     for q in (p1, p2, p3):
         pl.semaphore_signal(barrier, inc=1, device_id={"own": o, "rep": q}, device_id_type=MESH)
-    pl.semaphore_wait(barrier, n - 1 + 3)
-
-    w_copies = [
-        send(weight.at[at_cols(q)], wfull.at[:, at_part(r)], s_w.at[i], r_w.at[i], o, q)
-        for i, q in ((1, p2), (2, p3), (0, p1))
-    ]
-    meta_copies = [
-        send(meta, metas.at[o], s_meta.at[k - 1], r_meta.at[k - 1], lax.rem(o + k, n), r)
-        for k in range(1, n)
-    ]
-
+    for c in local:
+        c.start()
+    local[0].wait()
+    local[1].wait()
     below = lax.broadcasted_iota(jnp.int32, (samples, samples), 0)
     right = lax.broadcasted_iota(jnp.int32, (samples, samples), 1)
     upper = jnp.where(below < right, 1.0, 0.0).astype(BF16)
 
     def slots(ids):
-        out = jnp.zeros_like(ids)
-        for b in range(n):
-            out = jnp.where(ids == b, bmap[b], out)
-        return out
+        table = jnp.broadcast_to(meta[3:4, :], (n, samples))
+        return lane_pick(table, jnp.broadcast_to(ids, (n, samples)))[: ids.shape[0]]
 
     mine = meta[...]
     own_rank = ranks(slots(mine[0:1]), slots(mine[1:2]), n, upper)
@@ -102,21 +103,41 @@
     packed = jnp.dot(pack, hidden[...], preferred_element_type=F32).astype(BF16)
     for b in range(n):
         sendbuf[b] = packed[b * depth : (b + 1) * depth]
+    pl.semaphore_wait(barrier, n - 1 + 3)
+    hx = send(hidden_hbm, hidden_x, s_hx, r_hx, o, p2)
     row_copies = [
         send(sendbuf.at[lax.rem(o + k, n)], rows.at[at_rows(o), at_part(r)], s_row.at[k - 1], r_row.at[k - 1], lax.rem(o + k, n), r)
         for k in range(1, n)
     ]
+
+    w_copies = [
+        send(weight_hbm.at[at_cols(q)], wfull.at[:, at_part(r)], s_w.at[i], r_w.at[i], o, q)
+        for i, q in ((1, p2), (2, p3), (0, p1))
+    ]
+    meta_copies = [
+        send(meta_hbm, metas.at[o], s_meta.at[k - 1], r_meta.at[k - 1], lax.rem(o + k, n), r)
+        for k in range(1, n)
+    ]
+
     rows[at_rows(o), at_part(r)] = sendbuf[o]
-    wfull[:, at_part(r)] = weight[at_cols(r), :]
     metas[o] = mine
 
-    fx, fc, fr = [], [], []
+    hx.wait_recv()
+    packed_x = jnp.dot(pack, hidden_x[...], preferred_element_type=F32).astype(BF16)
+    for b in range(n):
+        sendbuf_x[b] = packed_x[b * depth : (b + 1) * depth]
+    rowx_copies = [
+        send(sendbuf_x.at[lax.rem(o + k, n)], rows.at[at_rows(o), at_part(p2)], s_rowx.at[k - 1], r_rowx.at[k - 1], lax.rem(o + k, n), r)
+        for k in range(1, n)
+    ]
+    rows[at_rows(o), at_part(p2)] = sendbuf_x[o]
+
+    fc, fr = [], []
     for k in range(n):
         s = lax.rem(o - k + n, n)
         if k > 0:
             row_copies[k - 1].wait_recv()
         block = rows.at[at_rows(s), at_part(r)]
-        fx.append(send(block, block, s_fx.at[k], r_fx.at[k], o, p2))
         fc.append(send(block, block, s_fc.at[k], r_fc.at[k], o, p1))
 
     for c in meta_copies:
@@ -155,8 +176,9 @@
     row_target = jnp.concatenate([(x[1:2] * 64.0 + x[2:3]) for x in infos], axis=1).astype(jnp.int32) - 1
 
     for k in range(n):
-        fx[k].wait_recv()
         s = lax.rem(o - k + n, n)
+        if k > 0:
+            rowx_copies[k - 1].wait_recv()
         block = rows.at[at_rows(s), at_part(p2)]
         fr.append(send(block, block, s_fr.at[k], r_fr.at[k], o, p1))
     for k in range(n):
@@ -165,6 +187,8 @@
         c.wait_recv()
     for k in range(n):
         fr[k].wait_recv()
+    local[2].wait()
+    local[3].wait()
 
     logits = lax.dot_general(wfull[...], rows[...], NT, preferred_element_type=F32)
     top = jnp.max(logits, axis=0, keepdims=True)
@@ -172,11 +196,19 @@
     hot = label_id == row_target
     target_sum = jnp.sum(jnp.where(hot, logits, 0.0), axis=0, keepdims=True)
     raised = jnp.exp(logits - top)
-    lt[...] = raised
+    e_all[at_cols(r), :] = raised.astype(BF16)
+    chunk = cols // 4
+    gx, gc, gr = [], [], []
+    for c in range(4):
+        block = e_all.at[at_cols(r, c, chunk)]
+        gx.append(send(block, block, s_gx.at[c], r_gx.at[c], o, p2))
+        gc.append(send(block, block, s_gc.at[c], r_gc.at[c], o, p1))
     lse = top + jnp.log(jnp.sum(raised, axis=0, keepdims=True))
     for sp in range(n // 2):
         stats[sp : sp + 1, :] = lse[:, sp * 128 : (sp + 1) * 128]
         stats[n // 2 + sp : n // 2 + sp + 1, :] = target_sum[:, sp * 128 : (sp + 1) * 128]
+        stats[n + sp : n + sp + 1, :] = top[:, sp * 128 : (sp + 1) * 128]
+    stats[n + n // 2 :, :] = jnp.zeros((n // 2, samples), F32)
     sr = [
         send(stats, statrep.at[r], s_sr.at[i], r_sr.at[i], o, q)
         for i, q in ((1, p2), (2, p3), (0, p1))
@@ -184,7 +216,7 @@
     statrep[r] = stats[...]
     for c in sr:
         c.wait_recv()
-    parts = [statrep[q] for q in range(4)]
+    parts = [statrep[q, 0:n, :] for q in range(4)]
     high = jnp.maximum(jnp.maximum(parts[0], parts[1]), jnp.maximum(parts[2], parts[3]))
     total = high + jnp.log(sum(jnp.exp(x - high) for x in parts))
     is_lse = lax.broadcasted_iota(jnp.int32, (n, samples), 0) < n // 2
@@ -213,17 +245,35 @@
             )
         norm_rows.append(jnp.where(lane < depth, pair[0], pair[1]))
     row_norm = jnp.concatenate(norm_rows, axis=1)
-    scale = jnp.where(row_valid, jnp.exp(top - row_norm), 0.0)
-
-    chunk = cols // 4
-    gx, gc, gr = [], [], []
+
+    def gradient(q, c, size):
+        at = at_cols(q, c, size)
+        tops = jnp.concatenate(
+            [statrep[pl.ds(q, 1), n + sp : n + sp + 1, :].reshape(1, samples) for sp in range(n // 2)], axis=1
+        )
+        scale = jnp.where(row_valid, jnp.exp(tops - row_norm), 0.0)
+        ids = lax.broadcasted_iota(jnp.int32, (size, row_count), 0) + (q * cols + c * size)
+        grad = e_all[at, :].astype(F32) * scale - jnp.where(ids == row_target, 1.0, 0.0)
+        g_all[at, :] = grad.astype(BF16)
+
+    def row_term(q, c, size):
+        at = at_cols(q, c, size)
+        gradient(q, c, size)
+        return lax.dot_general(g_all[at, :], weight[at, :], TN, preferred_element_type=F32)
+
+    def weight_term(q, i):
+        gw_ref[at_cols(q), :] = jnp.dot(
+            g_all[at_cols(q), :], rows[:, at_part(r)], preferred_element_type=F32
+        ).astype(BF16)
+        out = pltpu.make_async_copy(gw_ref.at[at_cols(q)], gw_hbm.at[at_cols(q)], s_loc.at[4 + i])
+        out.start()
+        outs.append(out)
+
+    outs = []
+    gh_acc[...] = row_term(r, 0, cols)
     for c in range(4):
-        ids = lax.broadcasted_iota(jnp.int32, (chunk, row_count), 0) + (r * cols + c * chunk)
-        grad = lt[c * chunk : (c + 1) * chunk, :] * scale - jnp.where(ids == row_target, 1.0, 0.0)
-        g_all[at_cols(r, c, chunk), :] = grad.astype(BF16)
-        block = g_all.at[at_cols(r, c, chunk)]
-        gx.append(send(block, block, s_gx.at[c], r_gx.at[c], o, p2))
-        gc.append(send(block, block, s_gc.at[c], r_gc.at[c], o, p1))
+        gc[c].wait_recv()
+    gh_acc[...] += row_term(p1, 0, cols)
 
     for sp in range(n // 2):
         held = statown[:, n // 2 + sp, :]
@@ -235,40 +285,30 @@
             tsums[s : s + 1, :] = jnp.sum(value, axis=0, keepdims=True)
     loss_ref[...] = norms[pl.ds(o, 1), :] - tsums[pl.ds(o, 1), :]
 
-    def row_term(q):
-        return lax.dot_general(g_all[at_cols(q), :], weight[at_cols(q), :], TN, preferred_element_type=F32)
-
-    def weight_term(q):
-        gw_ref[at_cols(q), :] = jnp.dot(
-            g_all[at_cols(q), :], rows[:, at_part(r)], preferred_element_type=F32
-        ).astype(BF16)
-
-    gh_acc[...] = row_term(r)
-    weight_term(r)
+    weight_term(r, 0)
+    weight_term(p1, 1)
     for c in range(4):
         gx[c].wait_recv()
-        block = g_all.at[at_cols(p2, c, chunk)]
+        block = e_all.at[at_cols(p2, c, chunk)]
         gr.append(send(block, block, s_gr.at[c], r_gr.at[c], o, p1))
-    for c in range(4):
-        gc[c].wait_recv()
-    gh_acc[...] += row_term(p1)
-    gh_acc[...] += row_term(p2)
+        gh_acc[...] += row_term(p2, c, chunk)
     for c in range(4):
         gr[c].wait_recv()
-    ghsend[...] = (gh_acc[...] + row_term(p3)).astype(BF16)
+    ghsend[...] = (gh_acc[...] + row_term(p3, 0, cols)).astype(BF16)
     back = [
         send(ghsend.at[at_rows(lax.rem(o + k, n))], ghrecv.at[at_rows(o)], s_gh.at[k - 1], r_gh.at[k - 1], lax.rem(o + k, n), r)
         for k in range(1, n)
     ]
     ghrecv[at_rows(o), :] = ghsend[at_rows(o), :]
-    weight_term(p1)
-    weight_term(p2)
-    weight_term(p3)
+    weight_term(p2, 2)
+    weight_term(p3, 3)
     for c in back:
         c.wait_recv()
     gh_ref[...] = lax.dot_general(pack, ghrecv[...], TN, preferred_element_type=F32)
     for c in pending:
         c.wait_send()
+    for c in outs:
+        c.wait()
 
 
 def fused(hidden, weight, bucket_map, active, label_pick):
@@ -279,44 +319,56 @@
     cols = labels // 4
     row_count = n * depth
     meta = jnp.concatenate(
-        [active.T, label_pick[None], jnp.zeros((5, samples), jnp.int32)], axis=0
+        [
+            active.T,
+            label_pick[None],
+            jnp.pad(bucket_map, (0, samples - n))[None],
+            jnp.zeros((4, samples), jnp.int32),
+        ],
+        axis=0,
     )
     vmem = pl.BlockSpec(memory_space=pltpu.VMEM)
     dma = pltpu.SemaphoreType.DMA
-    sems = []
-    for count in (n - 1, 3, n - 1, n, n, n, 3, n - 1, 4, 4, 4, n - 1):
+    sems = [dma((8,)), dma, dma]
+    for count in (n - 1, 3, n - 1, n - 1, n, n, 3, n - 1, 4, 4, 4, n - 1):
         sems += [dma((count,)), dma((count,))]
+    anyspace = pl.BlockSpec(memory_space=pl.ANY)
     loss, grad_hidden, grad_weight = pl.pallas_call(
-        functools.partial(kernel, n, depth, labels),
+        functools.partial(kernel, n, depth),
         out_shape=(
             jax.ShapeDtypeStruct((1, samples), F32),
             jax.ShapeDtypeStruct((samples, part), F32),
             jax.ShapeDtypeStruct((labels, part), BF16),
         ),
-        in_specs=[pl.BlockSpec(memory_space=pltpu.SMEM), vmem, vmem, vmem],
-        out_specs=(vmem, vmem, vmem),
+        in_specs=[anyspace, anyspace, anyspace],
+        out_specs=(vmem, vmem, anyspace),
         scratch_shapes=[
+            pltpu.VMEM((8, samples), jnp.int32),
+            pltpu.VMEM((samples, part), BF16),
+            pltpu.VMEM((samples, part), BF16),
+            pltpu.VMEM((labels, part), BF16),
             pltpu.VMEM((n, 8, samples), jnp.int32),
             pltpu.VMEM((cols, 4 * part), BF16),
             pltpu.VMEM((n, depth, part), BF16),
+            pltpu.VMEM((n, depth, part), BF16),
             pltpu.VMEM((row_count, 4 * part), BF16),
-            pltpu.VMEM((8, row_count), F32),
-            pltpu.VMEM((cols, row_count), F32),
-            pltpu.VMEM((n, samples), F32),
-            pltpu.VMEM((4, n, samples), F32),
+            pltpu.VMEM((2 * n, samples), F32),
+            pltpu.VMEM((4, 2 * n, samples), F32),
             pltpu.VMEM((n, samples), F32),
             pltpu.VMEM((n, n, samples), F32),
             pltpu.VMEM((n, samples), F32),
             pltpu.VMEM((n, samples), F32),
             pltpu.VMEM((labels, row_count), BF16),
+            pltpu.VMEM((labels, row_count), BF16),
             pltpu.VMEM((row_count, part), F32),
             pltpu.VMEM((row_count, part), BF16),
             pltpu.VMEM((row_count, part), BF16),
+            pltpu.VMEM((labels, part), BF16),
         ] + sems,
         compiler_params=pltpu.CompilerParams(
             collective_id=0, has_side_effects=True, vmem_limit_bytes=48 * 1024 * 1024
         ),
-    )(bucket_map, meta, hidden, weight[0])
+    )(meta, hidden, weight[0])
     return loss[0], grad_hidden, grad_weight[None]
 
 

time: 60.7 us -> 56.3 us (0.928)
  Pallas kernels: 53.3 us -> 49 us
    pallas_call x1, Pallas kernels: 53.3 us -> 49 us  [fused(): pl.pallas_call(functools.partial(kernel, n, depth), out_shape=(jax.ShapeD...]
where the time goes in v2:
time: 56.3 us; the launch traced here: 55.2 us
  Pallas kernels  49 us (87%)
  local copies, waits for them, and re-layouts  5.53 us (10%)
  between operations  0.66 us (1%)
    pallas_call x1, Pallas kernels, fused(): pl.pallas_call(functools.partial(kernel, n, depth), out_shape=(jax.ShapeD...  49 us
    unnamed x13, local copies, waits for them, and re-layouts  5.45 us

profile of v2, /device:TPU:0, one launch (start us, length us, event | category | flops | bytes accessed | tf_op | source)
XLA Modules:
  0.0 55.2 jit_solution(12304308131098261451)
XLA Ops:
  0.6 0.0 copy-start.4
  0.6 0.6 %copy-done.4 = s32[8]{0:T(128)S(1)} copy-done((s32[8]{0:T(128)S(1)}, s32[8]{0:T(128)}, u32[]{:S(2)}) %copy-start.4) | copy-done | bytes 56
  1.3 0.0 copy-start.2
  1.3 0.0 copy-start.3
  1.3 0.1 pad.8.clone
  1.4 0.6 %copy-done.2 = s32[128,2]{0,1:T(2,128)S(1)} copy-done((s32[128,2]{0,1:T(2,128)S(1)}, s32[128,2]{0,1:T(2,128)}, u32[]{:S(2)}) %copy-start.2) | copy-done | bytes 1048
  2.0 0.0 copy-done.3
  2.0 0.1 add_add_fusion.meta_hbm
  2.0 0.0 copy-start
  2.0 1.2 %copy-done = bf16[1,2048,256]{2,1,0:T(8,128)(2,1)S(1)} copy-done((bf16[1,2048,256]{2,1,0:T(8,128)(2,1)S(1)}, bf16[1,2048,256]{2,1,0:T(8,128)(2,1)}, u32[]{:S(2)}) %copy-start) | copy-done | bytes 1048600
  3.3 0.0 copy-start.1
  3.3 0.8 %copy-done.1 = bf16[128,256]{1,0:T(8,128)(2,1)S(1)} copy-done((bf16[128,256]{1,0:T(8,128)(2,1)S(1)}, bf16[128,256]{1,0:T(8,128)(2,1)}, u32[]{:S(2)}) %copy-start.1) | copy-done | bytes 65560
  4.1 49.0 %shard_map.76 = (f32[1,128]{1,0:T(1,128)S(1)}, f32[128,256]{1,0:T(8,128)S(1)}, bf16[2048,256]{1,0:T(8,128)(2,1)S(1)}) custom-call(s32[8,128]{1,0:T(8,128)S(1)} %add_add_fusion.meta_hbm, bf16[128,256]{1,0:T(8,128)(2,1)S(1)} %copy-done.1, bf16[2048,256]{1,0:T(8,128)(2,1)S(1)} %bitcast.7), custom_call_target="tpu_custom_call" | custom-call | tf_op jit(solution)/shard_map/pallas_call | solution.py:336
  53.1 0.5 copy.11
  53.6 0.7 %copy.12 = f32[128,256]{1,0:T(8,128)} copy(f32[128,256]{1,0:T(8,128)S(1)} %get-tuple-element.13) | data formatting | bytes 262144
  54.3 1.0 %copy.13 = bf16[1,2048,256]{2,1,0:T(8,128)(2,1)} copy(bf16[1,2048,256]{2,1,0:T(8,128)(2,1)S(1)} %bitcast.8) | data formatting | bytes 2097152
  (2 shorter events, 0.0 us)
Async XLA Ops:
  0.6 0.7 %copy-start.4 = (s32[8]{0:T(128)S(1)}, s32[8]{0:T(128)}, u32[]{:S(2)}) copy-start(s32[8]{0:T(128)} %param.7) | copy-start | bytes 100
  1.3 0.7 %copy-start.2 = (s32[128,2]{0,1:T(2,128)S(1)}, s32[128,2]{0,1:T(2,128)}, u32[]{:S(2)}) copy-start(s32[128,2]{0,1:T(2,128)} %param.8) | copy-start | bytes 3076
  1.3 0.7 %copy-start.3 = (s32[128]{0:T(128)S(1)}, s32[128]{0:T(128)}, u32[]{:S(2)}) copy-start(s32[128]{0:T(128)} %param.9) | copy-start | bytes 1540
  2.0 1.2 %copy-start = (bf16[1,2048,256]{2,1,0:T(8,128)(2,1)S(1)}, bf16[1,2048,256]{2,1,0:T(8,128)(2,1)}, u32[]{:S(2)}) copy-start(bf16[1,2048,256]{2,1,0:T(8,128)(2,1)} %param.6) | copy-start | bytes 3145732
  3.3 0.8 %copy-start.1 = (bf16[128,256]{1,0:T(8,128)(2,1)S(1)}, bf16[128,256]{1,0:T(8,128)(2,1)}, u32[]{:S(2)}) copy-start(bf16[128,256]{1,0:T(8,128)(2,1)} %hidden_hbm.1) | copy-start | bytes 196612

commit v3 on v2

--- a/solution.py
+++ b/solution.py
@@ -30,9 +30,9 @@
 
 
 def kernel(
-    n, depth, meta_hbm, hidden_hbm, weight_hbm,
+    n, depth, act_hbm, pick_hbm, map_hbm, hidden_hbm, weight_hbm,
     loss_ref, gh_ref, gw_hbm,
-    meta, hidden, hidden_x, weight, metas, wfull, sendbuf, sendbuf_x, rows, stats, statrep, comb, statown,
+    act, pick_own, table_in, meta, hidden, hidden_x, weight, metas, wfull, sendbuf, sendbuf_x, rows, stats, statrep, comb, statown,
     norms, tsums, e_all, g_all, gh_acc, ghsend, ghrecv, gw_ref,
     s_loc, s_hx, r_hx, s_meta, r_meta, s_w, r_w, s_row, r_row, s_rowx, r_rowx, s_fc, r_fc, s_fr, r_fr,
     s_sr, r_sr, s_so, r_so, s_gx, r_gx, s_gc, r_gc, s_gr, r_gr, s_gh, r_gh,
@@ -48,7 +48,7 @@
     row_count = n * depth
     pending = []
     local = [
-        pltpu.make_async_copy(meta_hbm, meta, s_loc.at[0]),
+        pltpu.make_async_copy(act_hbm, act, s_loc.at[0]),
         pltpu.make_async_copy(hidden_hbm, hidden, s_loc.at[1]),
         pltpu.make_async_copy(weight_hbm, weight, s_loc.at[2]),
         pltpu.make_async_copy(
@@ -56,6 +56,8 @@
             wfull.at[:, pl.ds(pl.multiple_of(r * part, part), part)],
             s_loc.at[3],
         ),
+        pltpu.make_async_copy(pick_hbm, pick_own, s_loc.at[8]),
+        pltpu.make_async_copy(map_hbm, table_in, s_loc.at[9]),
     ]
 
     def send(src, dst, ssem, rsem, own, rep):
@@ -85,6 +87,12 @@
     for c in local:
         c.start()
     local[0].wait()
+    local[4].wait()
+    local[5].wait()
+    meta[0:2, :] = act[...]
+    meta[2:3, :] = pick_own[...]
+    meta[3:8, :] = jnp.zeros((5, samples), jnp.int32)
+    meta[3:4, 0:n] = table_in[...]
     local[1].wait()
     below = lax.broadcasted_iota(jnp.int32, (samples, samples), 0)
     right = lax.broadcasted_iota(jnp.int32, (samples, samples), 1)
@@ -115,7 +123,7 @@
         for i, q in ((1, p2), (2, p3), (0, p1))
     ]
     meta_copies = [
-        send(meta_hbm, metas.at[o], s_meta.at[k - 1], r_meta.at[k - 1], lax.rem(o + k, n), r)
+        send(meta, metas.at[o], s_meta.at[k - 1], r_meta.at[k - 1], lax.rem(o + k, n), r)
         for k in range(1, n)
     ]
 
@@ -196,13 +204,6 @@
     hot = label_id == row_target
     target_sum = jnp.sum(jnp.where(hot, logits, 0.0), axis=0, keepdims=True)
     raised = jnp.exp(logits - top)
-    e_all[at_cols(r), :] = raised.astype(BF16)
-    chunk = cols // 4
-    gx, gc, gr = [], [], []
-    for c in range(4):
-        block = e_all.at[at_cols(r, c, chunk)]
-        gx.append(send(block, block, s_gx.at[c], r_gx.at[c], o, p2))
-        gc.append(send(block, block, s_gc.at[c], r_gc.at[c], o, p1))
     lse = top + jnp.log(jnp.sum(raised, axis=0, keepdims=True))
     for sp in range(n // 2):
         stats[sp : sp + 1, :] = lse[:, sp * 128 : (sp + 1) * 128]
@@ -213,6 +214,13 @@
         send(stats, statrep.at[r], s_sr.at[i], r_sr.at[i], o, q)
         for i, q in ((1, p2), (2, p3), (0, p1))
     ]
+    e_all[at_cols(r), :] = raised.astype(BF16)
+    chunk = cols // 4
+    gx, gc, gr = [], [], []
+    for c in range(4):
+        block = e_all.at[at_cols(r, c, chunk)]
+        gx.append(send(block, block, s_gx.at[c], r_gx.at[c], o, p2))
+        gc.append(send(block, block, s_gc.at[c], r_gc.at[c], o, p1))
     statrep[r] = stats[...]
     for c in sr:
         c.wait_recv()
@@ -318,21 +326,12 @@
     depth = 2 * samples * active.shape[1] // n
     cols = labels // 4
     row_count = n * depth
-    meta = jnp.concatenate(
-        [
-            active.T,
-            label_pick[None],
-            jnp.pad(bucket_map, (0, samples - n))[None],
-            jnp.zeros((4, samples), jnp.int32),
-        ],
-        axis=0,
-    )
     vmem = pl.BlockSpec(memory_space=pltpu.VMEM)
     dma = pltpu.SemaphoreType.DMA
-    sems = [dma((8,)), dma, dma]
+    sems = [dma((10,)), dma, dma]
     for count in (n - 1, 3, n - 1, n - 1, n, n, 3, n - 1, 4, 4, 4, n - 1):
         sems += [dma((count,)), dma((count,))]
-    anyspace = pl.BlockSpec(memory_space=pl.ANY)
+    hbm = pl.BlockSpec(memory_space=pltpu.HBM)
     loss, grad_hidden, grad_weight = pl.pallas_call(
         functools.partial(kernel, n, depth),
         out_shape=(
@@ -340,9 +339,12 @@
             jax.ShapeDtypeStruct((samples, part), F32),
             jax.ShapeDtypeStruct((labels, part), BF16),
         ),
-        in_specs=[anyspace, anyspace, anyspace],
-        out_specs=(vmem, vmem, anyspace),
+        in_specs=[hbm] * 5,
+        out_specs=(vmem, vmem, hbm),
         scratch_shapes=[
+            pltpu.VMEM((2, samples), jnp.int32),
+            pltpu.VMEM((1, samples), jnp.int32),
+            pltpu.VMEM((1, n), jnp.int32),
             pltpu.VMEM((8, samples), jnp.int32),
             pltpu.VMEM((samples, part), BF16),
             pltpu.VMEM((samples, part), BF16),
@@ -366,9 +368,9 @@
             pltpu.VMEM((labels, part), BF16),
         ] + sems,
         compiler_params=pltpu.CompilerParams(
-            collective_id=0, has_side_effects=True, vmem_limit_bytes=48 * 1024 * 1024
+            collective_id=0, has_side_effects=True, vmem_limit_bytes=60 * 1024 * 1024
         ),
-    )(meta, hidden, weight[0])
+    )(active.T, label_pick[None], bucket_map[None], hidden, weight[0])
     return loss[0], grad_hidden, grad_weight[None]
 
 

time: 56.3 us -> 49.7 us (0.88); the launches traced: 55.2 us -> 49.5 us
  Pallas kernels: 49 us -> 43.9 us
  local copies, waits for them, and re-layouts: 5.53 us -> 4.96 us
    pallas_call x1, Pallas kernels: 49 us -> 43.9 us  [fused(): pl.pallas_call(functools.partial(kernel, n, depth), out_shape=(jax.ShapeD...]
    unnamed x13 -> x5, local copies, waits for them, and re-layouts: 5.45 us -> 4.96 us
where the time goes in v3:
time: 49.7 us; the launch traced here: 49.5 us
  Pallas kernels  43.9 us (88%)
  local copies, waits for them, and re-layouts  4.96 us (10%)
  between operations  0.65 us (1%)
    pallas_call x1, Pallas kernels, fused(): pl.pallas_call(functools.partial(kernel, n, depth), out_shape=(jax.ShapeD...  43.9 us
    unnamed x5, local copies, waits for them, and re-layouts  4.96 us

profile of v3, /device:TPU:0, one launch (start us, length us, event | category | flops | bytes accessed | tf_op | source)
XLA Modules:
  0.0 49.5 jit_solution(7725058996666000102)
XLA Ops:
  0.6 43.9 %shard_map.76 = (f32[1,128]{1,0:T(1,128)}, f32[128,256]{1,0:T(8,128)}, bf16[2048,256]{1,0:T(8,128)(2,1)}) custom-call(s32[2,128]{1,0:T(2,128)} %bitcast.8, s32[1,128]{1,0:T(1,128)} %bitcast.9, s32[1,8]{1,0:T(1,128)} %bitcast.10, bf16[128,256]{1,0:T(8,128)(2,1)} %hidden_hbm.1, bf16[2048,256]{1,0:T(8,128)(2,1)} %bitcast.6), custom_call_target="tpu_custom_call" | custom-call | tf_op jit(solution)/shard_map/pallas_call | solution.py:335
  44.6 0.0 copy-start
  44.6 0.6 %copy-done = f32[1,128]{1,0:T(1,128)S(1)} copy-done((f32[1,128]{1,0:T(1,128)S(1)}, f32[1,128]{1,0:T(1,128)}, u32[]{:S(2)}) %copy-start) | copy-done | bytes 536
  45.2 0.5 %copy.11 = f32[128]{0:T(128)} copy(f32[128]{0:T(128)S(1)} %bitcast.11) | data formatting | bytes 1024
  45.7 1.6 %copy.12 = f32[128,256]{1,0:T(8,128)} copy(f32[128,256]{1,0:T(8,128)} %get-tuple-element.13) | data formatting | bytes 262144
  47.3 2.3 %copy.13 = bf16[1,2048,256]{2,1,0:T(8,128)(2,1)} copy(bf16[1,2048,256]{2,1,0:T(8,128)(2,1)} %bitcast.7) | data formatting | bytes 2097152
Async XLA Ops:
  44.6 0.6 %copy-start = (f32[1,128]{1,0:T(1,128)S(1)}, f32[1,128]{1,0:T(1,128)}, u32[]{:S(2)}) copy-start(f32[1,128]{1,0:T(1,128)} %get-tuple-element.6) | copy-start | bytes 1540

commit v4 on v3

--- a/solution.py
+++ b/solution.py
@@ -75,9 +75,12 @@
     def at_part(q):
         return pl.ds(pl.multiple_of(q * part, part), part)
 
-    def at_cols(q, c=0, size=None):
+    unit = cols // 4
+    pieces = ((0, unit), (unit, cols - unit))
+
+    def at_cols(q, start=0, size=None):
         size = cols if size is None else size
-        return pl.ds(pl.multiple_of(q * cols + c * size, size), size)
+        return pl.ds(pl.multiple_of(q * cols + start, unit), size)
 
     barrier = pltpu.get_barrier_semaphore()
     for k in range(1, n):
@@ -119,7 +122,11 @@
     ]
 
     w_copies = [
-        send(weight_hbm.at[at_cols(q)], wfull.at[:, at_part(r)], s_w.at[i], r_w.at[i], o, q)
+        send(
+            weight_hbm.at[at_cols(q, start, size)], wfull.at[start : start + size, at_part(r)],
+            s_w.at[3 * j + i], r_w.at[3 * j + i], o, q,
+        )
+        for j, (start, size) in enumerate(pieces)
         for i, q in ((1, p2), (2, p3), (0, p1))
     ]
     meta_copies = [
@@ -191,36 +198,46 @@
         fr.append(send(block, block, s_fr.at[k], r_fr.at[k], o, p1))
     for k in range(n):
         fc[k].wait_recv()
-    for c in w_copies:
-        c.wait_recv()
     for k in range(n):
         fr[k].wait_recv()
     local[2].wait()
     local[3].wait()
 
-    logits = lax.dot_general(wfull[...], rows[...], NT, preferred_element_type=F32)
-    top = jnp.max(logits, axis=0, keepdims=True)
-    label_id = lax.broadcasted_iota(jnp.int32, (cols, row_count), 0) + r * cols
-    hot = label_id == row_target
-    target_sum = jnp.sum(jnp.where(hot, logits, 0.0), axis=0, keepdims=True)
-    raised = jnp.exp(logits - top)
-    lse = top + jnp.log(jnp.sum(raised, axis=0, keepdims=True))
+    gx, gc, gr = [], [], []
+
+    def pass_on(c):
+        block = e_all.at[at_cols(r, c * unit, unit)]
+        gx.append(send(block, block, s_gx.at[c], r_gx.at[c], o, p2))
+        gc.append(send(block, block, s_gc.at[c], r_gc.at[c], o, p1))
+
+    tops, sums, targets = [], [], []
+    for j, (start, size) in enumerate(pieces):
+        for c in w_copies[3 * j : 3 * j + 3]:
+            c.wait_recv()
+        logits = lax.dot_general(wfull[start : start + size, :], rows[...], NT, preferred_element_type=F32)
+        top = jnp.max(logits, axis=0, keepdims=True)
+        label_id = lax.broadcasted_iota(jnp.int32, (size, row_count), 0) + (r * cols + start)
+        raised = jnp.exp(logits - top)
+        e_all[at_cols(r, start, size), :] = raised.astype(BF16)
+        if j == 0:
+            pass_on(0)
+        targets.append(jnp.sum(jnp.where(label_id == row_target, logits, 0.0), axis=0, keepdims=True))
+        sums.append(jnp.sum(raised, axis=0, keepdims=True))
+        tops.append(top)
+    target_sum = targets[0] + targets[1]
+    peak = jnp.maximum(tops[0], tops[1])
+    lse = peak + jnp.log(sums[0] * jnp.exp(tops[0] - peak) + sums[1] * jnp.exp(tops[1] - peak))
     for sp in range(n // 2):
         stats[sp : sp + 1, :] = lse[:, sp * 128 : (sp + 1) * 128]
         stats[n // 2 + sp : n // 2 + sp + 1, :] = target_sum[:, sp * 128 : (sp + 1) * 128]
-        stats[n + sp : n + sp + 1, :] = top[:, sp * 128 : (sp + 1) * 128]
-    stats[n + n // 2 :, :] = jnp.zeros((n // 2, samples), F32)
+        stats[n + sp : n + sp + 1, :] = tops[0][:, sp * 128 : (sp + 1) * 128]
+        stats[n + n // 2 + sp : n + n // 2 + sp + 1, :] = tops[1][:, sp * 128 : (sp + 1) * 128]
     sr = [
         send(stats, statrep.at[r], s_sr.at[i], r_sr.at[i], o, q)
         for i, q in ((1, p2), (2, p3), (0, p1))
     ]
-    e_all[at_cols(r), :] = raised.astype(BF16)
-    chunk = cols // 4
-    gx, gc, gr = [], [], []
-    for c in range(4):
-        block = e_all.at[at_cols(r, c, chunk)]
-        gx.append(send(block, block, s_gx.at[c], r_gx.at[c], o, p2))
-        gc.append(send(block, block, s_gc.at[c], r_gc.at[c], o, p1))
+    for c in range(1, 4):
+        pass_on(c)
     statrep[r] = stats[...]
     for c in sr:
         c.wait_recv()
@@ -254,19 +271,28 @@
         norm_rows.append(jnp.where(lane < depth, pair[0], pair[1]))
     row_norm = jnp.concatenate(norm_rows, axis=1)
 
-    def gradient(q, c, size):
-        at = at_cols(q, c, size)
-        tops = jnp.concatenate(
-            [statrep[pl.ds(q, 1), n + sp : n + sp + 1, :].reshape(1, samples) for sp in range(n // 2)], axis=1
+    def scale_of(q, j):
+        base = n + j * (n // 2)
+        high = jnp.concatenate(
+            [statrep[pl.ds(q, 1), base + sp : base + sp + 1, :].reshape(1, samples) for sp in range(n // 2)], axis=1
         )
-        scale = jnp.where(row_valid, jnp.exp(tops - row_norm), 0.0)
-        ids = lax.broadcasted_iota(jnp.int32, (size, row_count), 0) + (q * cols + c * size)
+        return jnp.where(row_valid, jnp.exp(high - row_norm), 0.0)
+
+    def gradient(q, start, size):
+        at = at_cols(q, start, size)
+        ids = lax.broadcasted_iota(jnp.int32, (size, row_count), 0) + (q * cols + start)
+        scale = scale_of(q, 0 if start == 0 else 1)
         grad = e_all[at, :].astype(F32) * scale - jnp.where(ids == row_target, 1.0, 0.0)
         g_all[at, :] = grad.astype(BF16)
 
-    def row_term(q, c, size):
-        at = at_cols(q, c, size)
-        gradient(q, c, size)
+    def row_term(q, start=0, size=None):
+        if size is None:
+            for first, length in pieces:
+                gradient(q, first, length)
+            at = at_cols(q)
+        else:
+            gradient(q, start, size)
+            at = at_cols(q, start, size)
         return lax.dot_general(g_all[at, :], weight[at, :], TN, preferred_element_type=F32)
 
     def weight_term(q, i):
@@ -278,10 +304,10 @@
         outs.append(out)
 
     outs = []
-    gh_acc[...] = row_term(r, 0, cols)
+    gh_acc[...] = row_term(r)
     for c in range(4):
         gc[c].wait_recv()
-    gh_acc[...] += row_term(p1, 0, cols)
+    gh_acc[...] += row_term(p1)
 
     for sp in range(n // 2):
         held = statown[:, n // 2 + sp, :]
@@ -297,12 +323,12 @@
     weight_term(p1, 1)
     for c in range(4):
         gx[c].wait_recv()
-        block = e_all.at[at_cols(p2, c, chunk)]
+        block = e_all.at[at_cols(p2, c * unit, unit)]
         gr.append(send(block, block, s_gr.at[c], r_gr.at[c], o, p1))
-        gh_acc[...] += row_term(p2, c, chunk)
+        gh_acc[...] += row_term(p2, c * unit, unit)
     for c in range(4):
         gr[c].wait_recv()
-    ghsend[...] = (gh_acc[...] + row_term(p3, 0, cols)).astype(BF16)
+    ghsend[...] = (gh_acc[...] + row_term(p3)).astype(BF16)
     back = [
         send(ghsend.at[at_rows(lax.rem(o + k, n))], ghrecv.at[at_rows(o)], s_gh.at[k - 1], r_gh.at[k - 1], lax.rem(o + k, n), r)
         for k in range(1, n)
@@ -319,6 +345,23 @@
         c.wait()
 
 
+def finish(loss_in, gh_in, gw_in, loss_out, gh_out, gw_out, loss_v, gh_v, gw_v, sem_in, sem_out):
+    step = gw_in.shape[0] // 4
+    moves = [(loss_in, loss_v, loss_out), (gh_in, gh_v, gh_out)]
+    for i in range(4):
+        at = pl.ds(i * step, step)
+        moves.append((gw_in.at[at], gw_v.at[at], gw_out.at[at]))
+    ins = [pltpu.make_async_copy(a, b, sem_in.at[i]) for i, (a, b, c) in enumerate(moves)]
+    outs = [pltpu.make_async_copy(b, c, sem_out.at[i]) for i, (a, b, c) in enumerate(moves)]
+    for c in ins:
+        c.start()
+    for c, d in zip(ins, outs):
+        c.wait()
+        d.start()
+    for c in outs:
+        c.wait()
+
+
 def fused(hidden, weight, bucket_map, active, label_pick):
     samples, part = hidden.shape
     labels = weight.shape[1]
@@ -329,7 +372,7 @@
     vmem = pl.BlockSpec(memory_space=pltpu.VMEM)
     dma = pltpu.SemaphoreType.DMA
     sems = [dma((10,)), dma, dma]
-    for count in (n - 1, 3, n - 1, n - 1, n, n, 3, n - 1, 4, 4, 4, n - 1):
+    for count in (n - 1, 6, n - 1, n - 1, n, n, 3, n - 1, 4, 4, 4, n - 1):
         sems += [dma((count,)), dma((count,))]
     hbm = pl.BlockSpec(memory_space=pltpu.HBM)
     loss, grad_hidden, grad_weight = pl.pallas_call(
@@ -371,6 +414,24 @@
             collective_id=0, has_side_effects=True, vmem_limit_bytes=60 * 1024 * 1024
         ),
     )(active.T, label_pick[None], bucket_map[None], hidden, weight[0])
+    loss, grad_hidden, grad_weight = pl.pallas_call(
+        finish,
+        out_shape=(
+            jax.ShapeDtypeStruct((1, samples), F32),
+            jax.ShapeDtypeStruct((samples, part), F32),
+            jax.ShapeDtypeStruct((labels, part), BF16),
+        ),
+        in_specs=[hbm] * 3,
+        out_specs=(hbm, hbm, hbm),
+        scratch_shapes=[
+            pltpu.VMEM((1, samples), F32),
+            pltpu.VMEM((samples, part), F32),
+            pltpu.VMEM((labels, part), BF16),
+            dma((6,)),
+            dma((6,)),
+        ],
+        compiler_params=pltpu.CompilerParams(vmem_limit_bytes=60 * 1024 * 1024),
+    )(loss, grad_hidden, grad_weight)
     return loss[0], grad_hidden, grad_weight[None]
 
 

time: 49.7 us -> 46.5 us (0.936)
  local copies, waits for them, and re-layouts: 4.96 us -> 0 us
  Pallas kernels: 43.9 us -> 45.7 us
    unnamed x5 -> x0, local copies, waits for them, and re-layouts: 4.96 us -> none
    pallas_call x0 -> x1, Pallas kernels: none -> 2.09 us  [fused(): pl.pallas_call(finish, out_shape=(jax.ShapeDtypeStruct((1, samples), F32)...]
where the time goes in v4:
time: 46.5 us; the launch traced here: 46.3 us
  Pallas kernels  45.7 us (98%)
  between operations  0.64 us (1%)
    pallas_call x1, Pallas kernels, fused(): pl.pallas_call(functools.partial(kernel, n, depth), out_shape=(jax.ShapeD...  43.6 us
    pallas_call x1, Pallas kernels, fused(): pl.pallas_call(finish, out_shape=(jax.ShapeDtypeStruct((1, samples), F32)...  2.09 us

profile of v4, /device:TPU:0, one launch (start us, length us, event | category | flops | bytes accessed | tf_op | source)
XLA Modules:
  0.0 46.3 jit_solution(2457301511927115551)
XLA Ops:
  0.6 43.6 %shard_map.76 = (f32[1,128]{1,0:T(1,128)}, f32[128,256]{1,0:T(8,128)}, bf16[2048,256]{1,0:T(8,128)(2,1)}) custom-call(s32[2,128]{1,0:T(2,128)} %bitcast.7, s32[1,128]{1,0:T(1,128)} %bitcast.8, s32[1,8]{1,0:T(1,128)} %bitcast.9, bf16[128,256]{1,0:T(8,128)(2,1)} %hidden_hbm.1, bf16[2048,256]{1,0:T(8,128)(2,1)} %bitcast.6), custom_call_target="tpu_custom_call" | custom-call | tf_op jit(solution)/shard_map/pallas_call | solution.py:378
  44.2 2.1 %shard_map.77 = (f32[1,128]{1,0:T(1,128)}, f32[128,256]{1,0:T(8,128)}, bf16[2048,256]{1,0:T(8,128)(2,1)}) custom-call(f32[1,128]{1,0:T(1,128)} %get-tuple-element.9.loss_in, f32[128,256]{1,0:T(8,128)} %get-tuple-element.10.gh_in, bf16[2048,256]{1,0:T(8,128)(2,1)} %get-tuple-element.11.gw_in), custom_call_target="tpu_custom_call" | custom-call | tf_op jit(solution)/shard_map/pallas_call | solution.py:417

commit v5 on v4

--- a/solution.py
+++ b/solution.py
@@ -326,9 +326,11 @@
         block = e_all.at[at_cols(p2, c * unit, unit)]
         gr.append(send(block, block, s_gr.at[c], r_gr.at[c], o, p1))
         gh_acc[...] += row_term(p2, c * unit, unit)
-    for c in range(4):
-        gr[c].wait_recv()
-    ghsend[...] = (gh_acc[...] + row_term(p3)).astype(BF16)
+        if c > 0:
+            gr[c - 1].wait_recv()
+            gh_acc[...] += row_term(p3, (c - 1) * unit, unit)
+    gr[3].wait_recv()
+    ghsend[...] = (gh_acc[...] + row_term(p3, 3 * unit, unit)).astype(BF16)
     back = [
         send(ghsend.at[at_rows(lax.rem(o + k, n))], ghrecv.at[at_rows(o)], s_gh.at[k - 1], r_gh.at[k - 1], lax.rem(o + k, n), r)
         for k in range(1, n)

time: 46.5 us -> 47 us (1.011)
    pallas_call x1, Pallas kernels: 43.6 us -> 44.1 us  [fused(): pl.pallas_call(functools.partial(kernel, n, depth), out_shape=(jax.ShapeD...]
where the time goes in v5:
time: 47 us; the launch traced here: 46.8 us
  Pallas kernels  46.1 us (98%)
  between operations  0.64 us (1%)
    pallas_call x1, Pallas kernels, fused(): pl.pallas_call(functools.partial(kernel, n, depth), out_shape=(jax.ShapeD...  44.1 us
    pallas_call x1, Pallas kernels, fused(): pl.pallas_call(finish, out_shape=(jax.ShapeDtypeStruct((1, samples), F32)...  2.09 us

profile of v5, /device:TPU:0, one launch (start us, length us, event | category | flops | bytes accessed | tf_op | source)
XLA Modules:
  0.0 46.8 jit_solution(14449791392030411677)
XLA Ops:
  0.6 44.1 %shard_map.76 = (f32[1,128]{1,0:T(1,128)}, f32[128,256]{1,0:T(8,128)}, bf16[2048,256]{1,0:T(8,128)(2,1)}) custom-call(s32[2,128]{1,0:T(2,128)} %bitcast.7, s32[1,128]{1,0:T(1,128)} %bitcast.8, s32[1,8]{1,0:T(1,128)} %bitcast.9, bf16[128,256]{1,0:T(8,128)(2,1)} %hidden_hbm.1, bf16[2048,256]{1,0:T(8,128)(2,1)} %bitcast.6), custom_call_target="tpu_custom_call" | custom-call | tf_op jit(solution)/shard_map/pallas_call | solution.py:380
  44.7 2.1 %shard_map.77 = (f32[1,128]{1,0:T(1,128)}, f32[128,256]{1,0:T(8,128)}, bf16[2048,256]{1,0:T(8,128)(2,1)}) custom-call(f32[1,128]{1,0:T(1,128)} %get-tuple-element.9.loss_in, f32[128,256]{1,0:T(8,128)} %get-tuple-element.10.gh_in, bf16[2048,256]{1,0:T(8,128)(2,1)} %get-tuple-element.11.gw_in), custom_call_target="tpu_custom_call" | custom-call | tf_op jit(solution)/shard_map/pallas_call | solution.py:419
